TPU v7x, 256 devices: a whole 4x4x8 slice. The times are simulated.
256 devices in a mesh: space: 32 (over x, z), col: 8 (over y, core).
Axes of the slice: x: 4, y: 4, z: 8, core: 2. Of those that a mesh axis runs over, the one named last changes fastest.
Arguments:
- blocks: bfloat16 [2560, 24, 128, 128], P('space', 'col'), may hold values from -0.109375 to 0.109375
- basis_tiles: bfloat16 [2560, 128, 128], P('space'), may hold values from -6 to 6
- weights: float32 [2560, 128], P('space'), may hold values from 0.1 to 1
- neighbour_device: int32 [2560, 24], P('space', 'col'), may hold values from 0 to 31, as said below
- neighbour_row: int32 [2560, 24], P('space', 'col'), may hold values from 0 to 79
- counts: int32 [2560], P('space'), may hold values from 12 to 24
- aggregate: int32 [2560], P('space'), may hold values from 0 to 9
- pair_slot: int32 [2560, 24], P('space', 'col'), may hold values from 0 to 3
Outputs:
- coarse: float32 [1280, 128, 128], P(('space', 'col'))
Inputs may be any that keep to these rules, and one draw needn't show every extreme that they name: `neighbour_device`: among the slots of one device's 80 rows that fall to one index of col, exactly 60 name another device; no other device is named more than 3 times there, and some other device exactly 3 times.
All inputs are finite; a program needn't handle non-finite values.
Results may differ from a plain program's by a relative error of at most 0.0045.
Values may be sent and summed in bfloat16 or wider, within the bound.
A program may use at most 128 MiB of HBM per device.

v0:
```python
import jax
import jax.numpy as jnp
from jax import lax
from jax.sharding import PartitionSpec as P

KC = 4
CAP = 3
NCD = 10


def per_device(
    blocks, basis_tiles, weights, neighbour_device, neighbour_row, counts, aggregate, pair_slot
):
    space_count = lax.axis_size("space")
    own_index = lax.axis_index("space")
    col_index = lax.axis_index("col")
    row_count, slot_count = neighbour_device.shape
    block_size = blocks.shape[2]
    coarse_size = basis_tiles.shape[2]
    slot_total = row_count * slot_count
    peer_of = neighbour_device.reshape(slot_total)
    row_of = neighbour_row.reshape(slot_total)
    remote = peer_of != own_index
    onehot = (
        (peer_of[:, None] == jnp.arange(space_count, dtype=jnp.int32)[None, :]) & remote[:, None]
    ).astype(jnp.int32)
    position = jnp.sum((jnp.cumsum(onehot, axis=0) - onehot) * onehot, axis=1)
    bucket = jnp.where(remote, peer_of * CAP + position, space_count * CAP)
    requests = jnp.zeros((space_count * CAP,), jnp.int32).at[bucket].set(row_of, mode="drop")
    requests = requests.reshape(space_count, CAP)
    asked_rows = lax.all_to_all(requests, "space", split_axis=0, concat_axis=0, tiled=True)
    tile_index = jnp.where(remote, row_count + bucket, row_of)
    received = lax.all_to_all(
        basis_tiles[asked_rows], "space", split_axis=0, concat_axis=0, tiled=True
    )
    tile_table = jnp.concatenate(
        [basis_tiles, received.reshape(space_count * CAP, block_size, coarse_size)], axis=0
    )
    fetched = tile_table[tile_index].reshape(row_count, slot_count, block_size, coarse_size)
    slot_number = col_index * slot_count + jnp.arange(slot_count, dtype=jnp.int32)
    usable = slot_number[None, :] < counts[:, None]
    masked = jnp.where(usable[:, :, None, None], blocks, jnp.zeros((), blocks.dtype))
    partial_sum = jnp.einsum("rkab,rkbc->rac", masked, fetched, preferred_element_type=jnp.float32)
    smoothed = lax.psum(partial_sum, "col")
    prolong = (basis_tiles.astype(jnp.float32) - weights[:, :, None] * smoothed).astype(
        jnp.bfloat16
    )
    received_prolong = lax.all_to_all(
        prolong[asked_rows], "space", split_axis=0, concat_axis=0, tiled=True
    )
    prolong_table = jnp.concatenate(
        [prolong, received_prolong.reshape(space_count * CAP, block_size, coarse_size)], axis=0
    )
    neighbour_prolong = prolong_table[tile_index].reshape(
        row_count, slot_count, block_size, coarse_size
    )
    applied = jnp.einsum(
        "rkab,rkbc->rkac", masked, neighbour_prolong, preferred_element_type=jnp.float32
    ).astype(jnp.bfloat16)
    contribution = jnp.einsum(
        "rad,rkae->rkde", prolong, applied, preferred_element_type=jnp.float32
    )
    targets = (aggregate[:, None] * KC + pair_slot).reshape(slot_total)
    coarse_local = jax.ops.segment_sum(
        contribution.reshape(slot_total, coarse_size, coarse_size), targets, num_segments=NCD * KC
    )
    return lax.psum_scatter(coarse_local, "col", scatter_dimension=0, tiled=True)


def solution(mesh):
    return jax.shard_map(
        per_device,
        mesh=mesh,
        in_specs=(
            P("space", "col", None, None),
            P("space", None, None),
            P("space", None),
            P("space", "col"),
            P("space", "col"),
            P("space"),
            P("space"),
            P("space", "col"),
        ),
        out_specs=P(("space", "col"), None, None),
        check_vma=False,
    )
```

profile of v0, /device:TPU:6, one launch (start us, length us, event | category | flops | bytes accessed | tf_op | source)
XLA Modules:
  0.0 429.6 jit_solution(17318623963266410459)
XLA Ops:
  6.5 0.8 copy.26
  7.3 0.7 broadcast_multiply_fusion
  8.0 0.8 copy.29
  8.8 0.2 reshape.182
  8.9 0.2 reshape.224
  9.1 0.2 eq.22
  9.2 0.7 broadcast_compare_fusion.1
  10.0 0.6 reduce-window.6
  10.6 0.2 slice_reduce_fusion
  10.8 0.1 bitcast_bitcast_fusion
  10.9 0.1 copy.24
  11.0 0.2 ne.29
  11.2 0.1 copy.25
  11.3 0.2 mul.47
  11.5 1.3 scatter_custom_fusion
  12.8 0.1 all_to_all.14
  12.9 19.3 %all_to_all.22 = s32[32,1,3]{2,1,0:T(1,128)S(1)} all-to-all(s32[32,1,3]{2,1,0:T(1,128)S(1)} %bitcast.44), channel_id=1, replica_groups=mesh['space'=32,'col'=8] {'space'}, dimensions={0} | all-to-all | bytes 768 | tf_op jit(solution)/shard_map/all_to_all | solution.py:31
  32.3 0.1 copy.31
  32.4 0.1 copy.32
  32.4 0.1 reshape.190
  32.6 0.0 copy-start.4
  32.6 0.0 copy-start.1
  32.6 4.6 %gather_fusion = bf16[96,128,128]{2,1,0:T(8,128)(2,1)} fusion(bf16[80,128,128]{2,1,0:T(8,128)(2,1)} %param.9, s32[1024]{0:T(1024)S(1)} %pad_clamp_fusion.1), kind=kCustom, calls=%fused_computation | custom fusion | bytes 6291840 | tf_op jit(solution)/shard_map/gather | solution.py:34
  37.2 6.6 %all-to-all-start.1 = ((bf16[32,3,128,128]{3,2,1,0:T(8,128)(2,1)}), bf16[32,3,128,128]{3,2,1,0:T(8,128)(2,1)}, u32[]{:S(2)}, u32[]{:S(2)}) async-start(bf16[32,3,128,128]{3,2,1,0:T(8,128)(2,1)} %bitcast.41), calls=%async_computation.1 | async-start | bytes 6291456 | tf_op jit(solution)/shard_map/all_to_all | solution.py:33
  43.9 0.0 all-reduce.3.cloned.1.call-start
  43.9 0.0 copy-done.4
  44.0 0.1 broadcast_compare_fusion
  44.0 71.3 %all-to-all-done.1 = bf16[32,3,128,128]{3,2,1,0:T(8,128)(2,1)} async-done(((bf16[32,3,128,128]{3,2,1,0:T(8,128)(2,1)}), bf16[32,3,128,128]{3,2,1,0:T(8,128)(2,1)}, u32[]{:S(2)}, u32[]{:S(2)}) %all-to-all-start.1) | async-done | bytes 3145760 | tf_op jit(solution)/shard_map/all_to_all | solution.py:33
  115.3 0.0 copy-done.1
  115.3 4.9 %pad_maximum_fusion = bf16[176,128,128]{2,1,0:T(8,128)(2,1)} fusion(bf16[96,128,128]{2,1,0:T(8,128)(2,1)} %bitcast.6, bf16[80,128,128]{2,1,0:T(8,128)(2,1)S(1)} %copy-done.1), kind=kLoop, calls=%fused_computation.11 | loop fusion | flops 2883584 | bytes 11534336 | tf_op jit(solution)/shard_map/concatenate | solution.py:36
  120.2 11.1 %gather_fusion.1 = bf16[240,128,128]{2,1,0:T(8,128)(2,1)} fusion(bf16[176,128,128]{2,1,0:T(8,128)(2,1)} %pad_maximum_fusion, s32[1024]{0:T(1024)S(1)} %pad_clamp_fusion), kind=kCustom, calls=%fused_computation.1 | custom fusion | bytes 15729600 | tf_op jit(solution)/shard_map/gather | solution.py:39
  131.4 0.0 copy-start.2
  131.4 10.1 %fusion.8 = f32[80,128,128]{2,1,0:T(8,128)} fusion(bf16[80,3,128,128]{3,2,1,0:T(8,128)(2,1)} %bitcast.43, bf16[80,3,128,128]{3,2,1,0:T(8,128)(2,1)} %param.8, pred[80,3]{1,0:T(8,128)(4,1)S(1)} %broadcast_compare_fusion), kind=kOutput, calls=%fused_computation.17 | convolution fusion | flops 1010565120 | bytes 20971760 | tf_op jit(solution)/shard_map/rkab,rkbc->rac/dot_general | solution.py:43
  141.4 0.0 all-reduce.3.cloned.1.call-update
  141.4 79.2 %all-reduce.3.cloned.1.call-done = f32[80,128,128]{2,1,0:T(8,128)} async-done(((f32[80,128,128]{2,1,0:T(8,128)}), f32[80,128,128]{2,1,0:T(8,128)}) %all-reduce.3.cloned.1.call-update) | async-done | bytes 5242896 | tf_op jit(solution)/shard_map/psum | solution.py:44
  220.7 0.0 copy-done.2
  220.7 4.6 %subtract_convert_fusion = bf16[80,128,128]{2,1,0:T(8,128)(2,1)S(1)} fusion(f32[80,128,128]{2,1,0:T(8,128)} %all-reduce.3.cloned.1.call-done, bf16[80,128,128]{2,1,0:T(8,128)(2,1)} %param.9, f32[80,128]{1,0:T(8,128)S(1)} %copy-done.2), kind=kLoop, calls=%fused_computation.13 | loop fusion | flops 5242880 | bytes 10526720 | tf_op jit(solution)/shard_map/convert_element_type | solution.py:45
  225.3 0.0 copy-start.5
  225.3 0.0 copy-start.3
  225.3 2.7 gather_fusion.2
  228.0 10.2 %all-to-all-start.2 = ((bf16[32,3,128,128]{3,2,1,0:T(8,128)(2,1)}), bf16[32,3,128,128]{3,2,1,0:T(8,128)(2,1)}, u32[]{:S(2)}, u32[]{:S(2)}) async-start(bf16[32,3,128,128]{3,2,1,0:T(8,128)(2,1)} %bitcast.42), calls=%async_computation.2 | async-start | bytes 6291456 | tf_op jit(solution)/shard_map/all_to_all | solution.py:48
  238.3 0.2 reduce-scatter.2.cloned.1.call-start
  238.5 0.0 copy-done.5
  238.5 0.0 copy-done.3
  238.5 0.1 copy.23
  238.6 0.2 reshape.230
  238.8 71.7 %all-to-all-done.2 = bf16[32,3,128,128]{3,2,1,0:T(8,128)(2,1)} async-done(((bf16[32,3,128,128]{3,2,1,0:T(8,128)(2,1)}), bf16[32,3,128,128]{3,2,1,0:T(8,128)(2,1)}, u32[]{:S(2)}, u32[]{:S(2)}) %all-to-all-start.2) | async-done | bytes 3145760 | tf_op jit(solution)/shard_map/all_to_all | solution.py:48
  310.5 4.9 %pad_maximum_fusion.1 = bf16[176,128,128]{2,1,0:T(8,128)(2,1)} fusion(bf16[96,128,128]{2,1,0:T(8,128)(2,1)} %bitcast.12, bf16[80,128,128]{2,1,0:T(8,128)(2,1)S(1)} %subtract_convert_fusion), kind=kLoop, calls=%fused_computation.12 | loop fusion | flops 2883584 | bytes 11534336 | tf_op jit(solution)/shard_map/concatenate | solution.py:51
  315.4 11.1 %gather_fusion.3 = bf16[240,128,128]{2,1,0:T(8,128)(2,1)} fusion(bf16[176,128,128]{2,1,0:T(8,128)(2,1)} %pad_maximum_fusion.1, s32[1024]{0:T(1024)S(1)} %pad_clamp_fusion), kind=kCustom, calls=%fused_computation.3 | custom fusion | bytes 15729600 | tf_op jit(solution)/shard_map/gather | solution.py:54
  326.5 11.1 %fusion = f32[80,3,128,128]{3,2,1,0:T(8,128)} fusion(bf16[80,3,128,128]{3,2,1,0:T(8,128)(2,1)} %bitcast.40, bf16[80,3,128,128]{3,2,1,0:T(8,128)(2,1)} %param.8, pred[80,3]{1,0:T(8,128)(4,1)S(1)} %broadcast_compare_fusion, bf16[80,128,128]{2,1,0:T(8,128)(2,1)S(1)} %subtract_convert_fusion), kind=kOutput, calls=%fused_computation.6 | convolution fusion | flops 2021130240 | bytes 34078960 | tf_op jit(solution)/shard_map/rad,rkae->rkde/dot_general | solution.py:60
  337.6 15.7 %copy.35 = f32[240,128,128]{2,1,0:T(8,128)} copy(f32[240,128,128]{1,2,0:T(8,128)} %bitcast.39) | data formatting | bytes 31457280 | tf_op jit(solution)/shard_map/reshape | solution.py:65
  353.3 0.3 broadcast_in_dim.20
  353.6 31.5 %scatter_fusion = f32[40,128,128]{2,1,0:T(8,128)S(1)} fusion(f32[40,128,128]{2,1,0:T(8,128)S(1)} %broadcast_in_dim.20, s32[240]{0:T(256)S(1)} %reshape.230, f32[240,128,128]{2,1,0:T(8,128)} %copy.35), kind=kCustom, calls=%fused_computation.5 | custom fusion | flops 3932160 | bytes 47186880 | tf_op jit(solution)/shard_map/scatter-add | solution.py:64
  385.1 0.0 copy-start
  385.1 1.5 copy-done
  386.6 0.0 reduce-scatter.2.cloned.1.call-update
  386.7 36.1 %reduce-scatter.2.cloned.1.call-done = f32[5,128,128]{2,1,0:T(8,128)} async-done(((f32[40,128,128]{2,1,0:T(8,128)}), f32[5,128,128]{2,1,0:T(8,128)}) %reduce-scatter.2.cloned.1.call-update) | async-done | bytes 327696 | tf_op jit(solution)/shard_map/reduce_scatter | solution.py:67
  (13 shorter events, 0.2 us)
Async XLA Ops:
  32.6 11.4 %copy-start.4 = (s32[80]{0:T(128)S(1)}, s32[80]{0:T(128)}, u32[]{:S(2)}) copy-start(s32[80]{0:T(128)} %param.13) | copy-start | bytes 964
  32.6 82.7 %copy-start.1 = (bf16[80,128,128]{2,1,0:T(8,128)(2,1)S(1)}, bf16[80,128,128]{2,1,0:T(8,128)(2,1)}, u32[]{:S(2)}) copy-start(bf16[80,128,128]{2,1,0:T(8,128)(2,1)} %param.9) | copy-start | bytes 7864324
  37.2 78.1 %all-to-all-start.1 = ((bf16[32,3,128,128]{3,2,1,0:T(8,128)(2,1)}), bf16[32,3,128,128]{3,2,1,0:T(8,128)(2,1)}, u32[]{:S(2)}, u32[]{:S(2)}) async-start(bf16[32,3,128,128]{3,2,1,0:T(8,128)(2,1)} %bitcast.41), calls=%async_computation.1 | async-start | bytes 6291456 | tf_op jit(solution)/shard_map/all_to_all | solution.py:33
  43.9 176.8 %all-reduce.3.cloned.1.call-start = ((), (), s32[]{:S(2)}) async-start(), calls=%async_computation.4 | async-start | bytes 10485760 | tf_op jit(solution)/shard_map/psum | solution.py:44
  131.4 89.3 %copy-start.2 = (f32[80,128]{1,0:T(8,128)S(1)}, f32[80,128]{1,0:T(8,128)}, u32[]{:S(2)}) copy-start(f32[80,128]{1,0:T(8,128)} %param.10) | copy-start | bytes 122884
  225.3 13.2 %copy-start.5 = (s32[80]{0:T(128)S(1)}, s32[80]{0:T(128)}, u32[]{:S(2)}) copy-start(s32[80]{0:T(128)} %param.14) | copy-start | bytes 964
  225.3 13.2 %copy-start.3 = (s32[80,3]{0,1:T(4,128)S(1)}, s32[80,3]{0,1:T(4,128)}, u32[]{:S(2)}) copy-start(s32[80,3]{0,1:T(4,128)} %param.15) | copy-start | bytes 2884
  228.0 82.5 %all-to-all-start.2 = ((bf16[32,3,128,128]{3,2,1,0:T(8,128)(2,1)}), bf16[32,3,128,128]{3,2,1,0:T(8,128)(2,1)}, u32[]{:S(2)}, u32[]{:S(2)}) async-start(bf16[32,3,128,128]{3,2,1,0:T(8,128)(2,1)} %bitcast.42), calls=%async_computation.2 | async-start | bytes 6291456 | tf_op jit(solution)/shard_map/all_to_all | solution.py:48
  238.3 184.5 %reduce-scatter.2.cloned.1.call-start = ((), (), s32[]{:S(2)}) async-start(), calls=%async_computation.5 | async-start | bytes 2949120 | tf_op jit(solution)/shard_map/reduce_scatter | solution.py:67
  385.1 1.5 copy-start
Sparse Core Ops, SparseCore 0:
  141.6 79.0 all-reduce.2
  386.8 35.9 reduce-scatter.1
where the time goes:
time: 431 us; the launch traced here: 430 us
  waiting for transfers between devices  258 us (60%)
  local copies, waits for them, and re-layouts  51.8 us (12%)
  other arithmetic  48.2 us (11%)
  matrix products  21.2 us (5%)
  blocking collectives  19.3 us (4%)
  starting transfers between devices  17.1 us (4%)
  between operations  13.6 us (3%)
    psum x1, waiting for transfers between devices, per_device(): smoothed = lax.psum(partial_sum, 'col')  79.2 us
    all_to_all x1, waiting for transfers between devices, per_device(): lax.all_to_all(prolong[asked_rows], 'space', split_axis=0, concat_axis=0,...  71.7 us
    all_to_all x1, waiting for transfers between devices, per_device(): lax.all_to_all(basis_tiles[asked_rows], 'space', split_axis=0, concat_axi...  71.3 us
    reduce_scatter x1, waiting for transfers between devices, per_device(): lax.psum_scatter(coarse_local, 'col', scatter_dimension=0, tiled=True)  36.1 us
    scatter-add x1, other arithmetic, per_device(): jax.ops.segment_sum(contribution.reshape(slot_total, coarse_size, coarse_...  31.5 us
    all_to_all x1, blocking collectives, per_device(): lax.all_to_all(requests, 'space', split_axis=0, concat_axis=0, tiled=True)  19.3 us
    reshape x1, local copies, waits for them, and re-layouts, per_device(): contribution.reshape(slot_total, coarse_size, coarse_size)  15.7 us
    gather x1, local copies, waits for them, and re-layouts, per_device(): prolong_table[tile_index]  11.1 us
  transfers between devices with their start and end apart: 4, of which 4 were waited for; matrix products, arithmetic and copies ran while one was open for 0% of the time, Pallas kernels for 0%

commit v1 on v0

v1 whole, which is shorter than its diff:
```python
import functools

import jax
import jax.numpy as jnp
from jax import lax
from jax.experimental import pallas as pl
from jax.experimental.pallas import tpu as pltpu
from jax.sharding import PartitionSpec as P

KC = 4
CAP = 3
NCD = 10
NX, NZ, NY = 4, 8, 4
MESH = pl.DeviceIdType.MESH
F32 = jnp.float32
BF16 = jnp.bfloat16


def dot(a, b):
    return jnp.dot(a, b, preferred_element_type=F32)


def dot_t(a, b):
    return lax.dot_general(a, b, (((0,), (0,)), ((), ())), preferred_element_type=F32)


def step_offset(o):
    zi, xi = o // NX, o % NX
    hz, hx = (zi + 1) // 2, (xi + 1) // 2
    dz = ((zi % 2) * hz + (1 - zi % 2) * (NZ - hz)) % NZ
    dx = ((xi % 2) * hx + (1 - xi % 2) * (NX - hx)) % NX
    return dx, dz


def kernel(
    sizes,
    tab,
    req,
    weights,
    blocks_hbm,
    basis_hbm,
    out,
    blocks,
    basis,
    ptab,
    asked_v,
    asked,
    stage,
    recv1,
    recv2,
    big,
    total,
    xs,
    xr,
    s1,
    r1,
    s2,
    r2,
    xs_f,
    xr_f,
    s1_f,
    r1_f,
    s2_f,
    r2_f,
    load_sem,
    req_send,
    req_recv,
    a_send,
    a_recv,
    b_send,
    b_recv,
    rs_send,
    rs_recv,
    rf_send,
    rf_recv,
    ag_send,
    ag_recv,
):
    rows, slots, n_local = sizes
    space_count = NX * NZ
    peers = space_count - 1
    own_rows = rows // (2 * NY)
    lidx_at, ridx_at = 0, slots
    slot_at = 2 * slots
    loc_at = slot_at + space_count * CAP
    rem_at = loc_at + n_local
    n_remote = slots - n_local
    last_l_at = rem_at + n_remote
    last_r_at = last_l_at + NCD * KC
    r_base = rows
    c_base = n_local
    g_base = n_local + space_count * CAP

    me = lax.axis_index("space")
    col = lax.axis_index("col")
    mx, mz = me // NZ, me % NZ
    my, core = col // 2, col % 2
    ya = my + 1 - 2 * (my % 2)
    yb = NY - 1 - my
    yo = (my + 2) % NY
    dev_x = (me, my * 2 + 1 - core)
    dev_a = (me, ya * 2 + core)
    dev_b = (me, yb * 2 + core)

    def target(o):
        dx, dz = step_offset(o)
        return (((mx + dx) % NX) * NZ + (mz + dz) % NZ, col)

    def origin(o):
        dx, dz = step_offset(o)
        return (((mx + NX - dx) % NX) * NZ + (mz + NZ - dz) % NZ, col)

    load_a = pltpu.make_async_copy(blocks_hbm, blocks, load_sem.at[0])
    load_b = pltpu.make_async_copy(basis_hbm, basis.at[pl.ds(0, rows)], load_sem.at[1])
    load_b.start()
    load_a.start()

    barrier = pltpu.get_barrier_semaphore()

    def greet(o, carry):
        pl.semaphore_signal(barrier, 1, device_id=target(o), device_id_type=MESH)
        return carry

    lax.fori_loop(1, space_count, greet, 0)
    for peer in (dev_x, dev_a, dev_b):
        pl.semaphore_signal(barrier, 1, device_id=peer, device_id_type=MESH)
    zero_b = jnp.zeros((128, 128), BF16)
    zero_f = jnp.zeros((128, 128), F32)
    basis[rows] = zero_b
    ptab[rows] = zero_b
    big[r_base] = zero_f
    big[c_base] = zero_f
    pl.semaphore_wait(barrier, peers + 3)

    def remote(src, dst, send, recv, dev):
        return pltpu.make_async_remote_copy(
            src, dst, send, recv, device_id=dev, device_id_type=MESH
        )

    def ask(o):
        return remote(req.at[o], asked_v.at[o], req_send.at[o], req_recv.at[o], origin(o))

    def ask_start(o, carry):
        ask(o).start()
        return carry

    lax.fori_loop(1, space_count, ask_start, 0)

    def ask_wait(o, carry):
        ask(o).wait()
        return carry

    lax.fori_loop(1, space_count, ask_wait, 0)
    to_scalar = pltpu.make_async_copy(
        asked_v.at[pl.ds(1, peers)], asked.at[pl.ds(1, peers)], load_sem.at[2]
    )
    to_scalar.start()
    to_scalar.wait()
    load_b.wait()

    def halo1(o):
        return remote(stage.at[o], recv1.at[o], a_send.at[o], a_recv.at[o], target(o))

    def halo2(o):
        return remote(stage.at[o], recv2.at[o], b_send.at[o], b_recv.at[o], target(o))

    def send1(o, carry):
        for j in range(CAP):
            stage[o, j] = basis[asked[o, 0, j]]
        halo1(o).start()
        return carry

    lax.fori_loop(1, space_count, send1, 0)
    load_a.wait()

    def local_smooth(i, carry):
        lhs = jnp.concatenate([blocks[3 * i + k] for k in range(3)], axis=1)
        rhs = jnp.concatenate([basis[tab[lidx_at + 3 * i + k]] for k in range(3)], axis=0)
        big[i] = dot(lhs, rhs)
        return carry

    lax.fori_loop(0, rows, local_smooth, 0, unroll=2)

    def remote_smooth(o, carry):
        halo1(o).wait_recv()
        for j in range(CAP):
            big[r_base + o * CAP + j] = dot(blocks[tab[slot_at + o * CAP + j]], recv1[o, j])
        return carry

    lax.fori_loop(1, space_count, remote_smooth, 0)

    def reduce_scatter(n, part, xs, xr, s1, r1, s2, r2, send, recv):
        groups = (ya, yb, yo, my)
        h1 = (n + 1) // 2
        h2 = n - h1

        def swap(i):
            return remote(
                xs.at[pl.ds(i * n, n)], xr.at[pl.ds(i * n, n)], send.at[i], recv.at[i], dev_x
            )

        for i in range(4):

            def fill(t, carry):
                xs[i * n + t] = part((groups[i] * 2 + 1 - core) * n + t).astype(BF16)
                return carry

            lax.fori_loop(0, n, fill, 0)
            swap(i).start()
        for i in range(4):

            def keep(t, carry):
                total[i * n + t] = part((groups[i] * 2 + core) * n + t)
                return carry

            lax.fori_loop(0, n, keep, 0)

        def hop(src, dst, at, size, sem, dev):
            return remote(
                src.at[pl.ds(at, size)], dst.at[pl.ds(at, size)], send.at[sem], recv.at[sem], dev
            )

        m0 = hop(s1, r1, 0, h1, 4, dev_a)
        m1 = hop(s1, r1, h1, h1, 5, dev_a)
        m2 = hop(s1, r1, 2 * h1, h2, 6, dev_b)
        m3 = hop(s1, r1, 2 * h1 + h2, h2, 7, dev_b)
        m4 = hop(s2, r2, 0, h1, 8, dev_b)
        m5 = hop(s2, r2, h1, h2, 9, dev_a)

        def add_swapped(i):
            swap(i).wait_recv()

            def add(t, carry):
                total[i * n + t] += xr[i * n + t].astype(F32)
                return carry

            lax.fori_loop(0, n, add, 0)

        def put(dst, at, first, size):
            def one(t, carry):
                dst[at + t] = total[first + t].astype(BF16)
                return carry

            lax.fori_loop(0, size, one, 0)

        def take(src, at, first, size):
            def one(t, carry):
                total[first + t] += src[at + t].astype(F32)
                return carry

            lax.fori_loop(0, size, one, 0)

        add_swapped(0)
        put(s1, 0, 0, h1)
        m0.start()
        add_swapped(1)
        put(s1, 2 * h1, n + h1, h2)
        m2.start()
        add_swapped(2)
        put(s1, h1, 2 * n, h1)
        m1.start()
        put(s1, 2 * h1 + h2, 2 * n + h1, h2)
        m3.start()
        add_swapped(3)
        m1.wait_recv()
        take(r1, h1, n, h1)
        put(s2, 0, n, h1)
        m4.start()
        m3.wait_recv()
        take(r1, 2 * h1 + h2, h1, h2)
        put(s2, h1, h1, h2)
        m5.start()
        m0.wait_recv()
        take(r1, 0, 3 * n, h1)
        m2.wait_recv()
        take(r1, 2 * h1, 3 * n + h1, h2)
        m4.wait_recv()
        take(r2, 0, 3 * n, h1)
        m5.wait_recv()
        take(r2, h1, 3 * n + h1, h2)

        def drain():
            for i in range(4):
                swap(i).wait_send()
            for m in (m0, m1, m2, m3, m4, m5):
                m.wait_send()

        return drain

    def smooth_part(row):
        acc = big[row]
        for k in range(3):
            acc = acc + big[r_base + tab[ridx_at + 3 * row + k]]
        return acc

    drain1 = reduce_scatter(own_rows, smooth_part, xs, xr, s1, r1, s2, r2, rs_send, rs_recv)

    n = own_rows
    h1 = (n + 1) // 2
    h2 = n - h1

    def make_prolong(t, carry):
        row = col * n + t
        scale = jnp.broadcast_to(weights[row], (128, 128)).T
        ptab[row] = (basis[row].astype(F32) - scale * total[3 * n + t]).astype(BF16)
        return carry

    lax.fori_loop(0, n, make_prolong, 0)

    def spread(y, at, size, sem, dev):
        region = ptab.at[pl.ds((y * 2 + core) * n + at, size)]
        return remote(region, region, ag_send.at[sem], ag_recv.at[sem], dev)

    def arrive(y, c, at, size, sem):
        region = ptab.at[pl.ds((y * 2 + c) * n + at, size)]
        return remote(region, region, ag_send.at[sem], ag_recv.at[sem], dev_x)

    g0 = spread(my, 0, n, 0, dev_a)
    g1 = spread(my, 0, n, 1, dev_b)
    g2 = spread(my, 0, n, 2, dev_x)
    g0.start()
    g1.start()
    g2.start()
    arrive(ya, core, 0, n, 0).wait_recv()
    g3 = spread(ya, 0, h1, 3, dev_b)
    g3.start()
    g5 = spread(ya, 0, n, 5, dev_x)
    g5.start()
    arrive(yb, core, 0, n, 1).wait_recv()
    g4 = spread(yb, h1, h2, 4, dev_a)
    g4.start()
    g6 = spread(yb, 0, n, 6, dev_x)
    g6.start()
    arrive(yo, core, 0, h1, 3).wait_recv()
    g7 = spread(yo, 0, h1, 7, dev_x)
    g7.start()
    arrive(yo, core, h1, h2, 4).wait_recv()
    g8 = spread(yo, h1, h2, 8, dev_x)
    g8.start()

    def drain_halo1(o, carry):
        halo1(o).wait_send()
        return carry

    lax.fori_loop(1, space_count, drain_halo1, 0)
    other = 1 - core
    arrive(my, other, 0, n, 2).wait_recv()
    arrive(ya, other, 0, n, 5).wait_recv()
    arrive(yb, other, 0, n, 6).wait_recv()
    arrive(yo, other, 0, h1, 7).wait_recv()
    arrive(yo, other, h1, h2, 8).wait_recv()

    def send2(o, carry):
        for j in range(CAP):
            stage[o, j] = ptab[asked[o, 0, j]]
        halo2(o).start()
        return carry

    lax.fori_loop(1, space_count, send2, 0)
    drain1()
    for g in (g0, g1, g2, g3, g4, g5, g6, g7, g8):
        g.wait_send()

    def galerkin(slot, tile):
        applied = dot(blocks[slot], tile).astype(BF16)
        return dot_t(ptab[lax.div(slot, 3)], applied)

    group = 4

    def local_galerkin(b, acc):
        parts = []
        for u in range(group):
            code = tab[loc_at + b * group + u]
            parts.append((code >> 15, galerkin(code & 255, ptab[(code >> 8) & 127])))
        for u, (keep, c) in enumerate(parts):
            acc = jnp.where(keep > 0, acc, 0.0) + c
            big[b * group + u] = acc
        return acc

    lax.fori_loop(0, n_local // group, local_galerkin, zero_f)

    def remote_galerkin(o, carry):
        halo2(o).wait_recv()
        for j in range(CAP):
            big[c_base + o * CAP + j] = galerkin(tab[slot_at + o * CAP + j], recv2[o, j])
        return carry

    lax.fori_loop(1, space_count, remote_galerkin, 0)

    def remote_sum(q, acc):
        code = tab[rem_at + q]
        acc = jnp.where((code >> 15) > 0, acc, 0.0) + big[c_base + (code & 127)]
        big[g_base + q] = acc
        return acc

    lax.fori_loop(0, n_remote, remote_sum, zero_f, unroll=4)

    def coarse_part(t):
        return big[tab[last_l_at + t]] + big[tab[last_r_at + t]]

    n_out = NCD * KC // (2 * NY)
    drain2 = reduce_scatter(
        n_out, coarse_part, xs_f, xr_f, s1_f, r1_f, s2_f, r2_f, rf_send, rf_recv
    )
    for t in range(n_out):
        out[t] = total[3 * n_out + t]

    def drain_halo2(o, carry):
        halo2(o).wait_send()
        return carry

    lax.fori_loop(1, space_count, drain_halo2, 0)
    drain2()


def ring_rank(delta, size):
    return jnp.where(delta == 0, 0, jnp.where(2 * delta <= size, 2 * delta - 1, 2 * (size - delta)))


def per_device(
    blocks, basis_tiles, weights, neighbour_device, neighbour_row, counts, aggregate, pair_slot
):
    own = lax.axis_index("space")
    col = lax.axis_index("col")
    space_count = lax.axis_size("space")
    rows, slot_count = neighbour_device.shape
    slots = rows * slot_count
    n_remote = 60
    n_local = slots - n_remote
    peer = neighbour_device.reshape(slots)
    row_of = neighbour_row.reshape(slots)
    remote = peer != own
    live = (
        col * slot_count + jnp.arange(slot_count, dtype=jnp.int32)[None, :] < counts[:, None]
    ).reshape(slots)
    target = (aggregate[:, None] * KC + pair_slot).reshape(slots)
    step = ring_rank((own % NZ - peer % NZ) % NZ, NZ) * NX + ring_rank(
        (own // NZ - peer // NZ) % NX, NX
    )
    ids = jnp.arange(slots, dtype=jnp.int32)
    earlier = ids[None, :] < ids[:, None]
    position = jnp.sum((step[None, :] == step[:, None]) & earlier, axis=1, dtype=jnp.int32)
    bucket = jnp.where(remote, step * CAP + position, 0)
    buckets = jnp.arange(space_count * CAP, dtype=jnp.int32)
    hit = (bucket[None, :] == buckets[:, None]) & remote[None, :]
    packed = jnp.sum(jnp.where(hit, (row_of + 128 * ids)[None, :], 0), axis=1, dtype=jnp.int32)
    lidx = jnp.where(remote | ~live, rows, row_of)
    ridx = jnp.where(live, bucket, 0)
    before = (target[None, :] < target[:, None]) | ((target[None, :] == target[:, None]) & earlier)
    same = (target[None, :] == target[:, None]) & earlier
    kind = remote[None, :] == remote[:, None]
    rank = jnp.sum(before & kind, axis=1, dtype=jnp.int32)
    keep = jnp.any(same & kind, axis=1).astype(jnp.int32)
    code = jnp.where(remote, ridx, ids + 256 * lidx) + (keep << 15)
    place = jnp.where(remote, n_local + rank, rank)
    ordered = jnp.sum(
        jnp.where(place[None, :] == ids[:, None], code[None, :], 0), axis=1, dtype=jnp.int32
    )
    targets = jnp.arange(NCD * KC, dtype=jnp.int32)
    upto = target[None, :] <= targets[:, None]
    equal = target[None, :] == targets[:, None]

    def last(mine, base):
        count = jnp.sum(upto & mine[None, :], axis=1, dtype=jnp.int32)
        some = jnp.any(equal & mine[None, :], axis=1)
        return jnp.where(some, base + count - 1, n_local)

    tab = jnp.concatenate(
        [
            lidx,
            ridx,
            packed >> 7,
            ordered,
            last(~remote, 0),
            last(remote, n_local + space_count * CAP),
        ]
    )
    req = jnp.broadcast_to(
        jnp.pad((packed & 127).reshape(space_count, 1, CAP), ((0, 0), (0, 0), (0, 128 - CAP))),
        (space_count, 8, 128),
    )
    own_rows = rows // (2 * NY)
    n_out = NCD * KC // (2 * NY)
    tile = (128, 128)

    def rs_buffers(n):
        h1 = (n + 1) // 2
        return [
            pltpu.VMEM((4 * n,) + tile, BF16),
            pltpu.VMEM((4 * n,) + tile, BF16),
            pltpu.VMEM((2 * n,) + tile, BF16),
            pltpu.VMEM((2 * n,) + tile, BF16),
            pltpu.VMEM((n,) + tile, BF16),
            pltpu.VMEM((n,) + tile, BF16),
        ]

    dma = pltpu.SemaphoreType.DMA
    return pl.pallas_call(
        functools.partial(kernel, (rows, slots, n_local)),
        out_shape=jax.ShapeDtypeStruct((n_out,) + tile, F32),
        in_specs=[
            pl.BlockSpec(memory_space=pltpu.SMEM),
            pl.BlockSpec(memory_space=pltpu.VMEM),
            pl.BlockSpec(memory_space=pltpu.VMEM),
            pl.BlockSpec(memory_space=pl.ANY),
            pl.BlockSpec(memory_space=pl.ANY),
        ],
        out_specs=pl.BlockSpec(memory_space=pltpu.VMEM),
        scratch_shapes=[
            pltpu.VMEM((slots,) + tile, BF16),
            pltpu.VMEM((rows + 1,) + tile, BF16),
            pltpu.VMEM((rows + 1,) + tile, BF16),
            pltpu.VMEM((space_count, 8, 128), jnp.int32),
            pltpu.SMEM((space_count, 8, 128), jnp.int32),
            pltpu.VMEM((space_count, CAP) + tile, BF16),
            pltpu.VMEM((space_count, CAP) + tile, BF16),
            pltpu.VMEM((space_count, CAP) + tile, BF16),
            pltpu.VMEM((n_local + space_count * CAP + n_remote,) + tile, F32),
            pltpu.VMEM((4 * own_rows,) + tile, F32),
            *rs_buffers(own_rows),
            *rs_buffers(n_out),
            dma((3,)),
            *([dma((space_count,))] * 6),
            *([dma((10,))] * 4),
            *([dma((9,))] * 2),
        ],
        compiler_params=pltpu.CompilerParams(
            collective_id=0, has_side_effects=True, vmem_limit_bytes=62 << 20
        ),
        name="galerkin_step",
    )(
        tab,
        req,
        weights.reshape(rows, 1, 128),
        blocks.reshape((slots,) + tile),
        basis_tiles,
    )


def solution(mesh):
    return jax.shard_map(
        per_device,
        mesh=mesh,
        in_specs=(
            P("space", "col", None, None),
            P("space", None, None),
            P("space", None),
            P("space", "col"),
            P("space", "col"),
            P("space"),
            P("space"),
            P("space", "col"),
        ),
        out_specs=P(("space", "col"), None, None),
        check_vma=False,
    )
```

time: 431 us -> 229 us (0.53)
  waiting for transfers between devices: 258 us -> 0 us
  Pallas kernels: 0 us -> 220 us
  local copies, waits for them, and re-layouts: 51.8 us -> 5.43 us
  other arithmetic: 48.2 us -> 3.14 us
  matrix products: 21.2 us -> 0 us
  blocking collectives: 19.3 us -> 0 us
  starting transfers between devices: 17.1 us -> 0 us
  between operations: 13.6 us -> 0.08 us
    pallas_call x0 -> x1, Pallas kernels: none -> 220 us  [per_device(): pl.pallas_call(functools.partial(kernel, (rows, slots, n_local)), out_sha...]
    all_to_all x2 -> x0, waiting for transfers between devices: 143 us -> none  [the longest x1 71.7 us: per_device(): lax.all_to_all(prolong[asked_rows], 'space', split_axis=0, concat_axis=0,...]
    psum x1 -> x0, waiting for transfers between devices: 79.2 us -> none  [per_device(): smoothed = lax.psum(partial_sum, 'col')]
    reduce_scatter x1 -> x0, waiting for transfers between devices: 36.1 us -> none  [per_device(): lax.psum_scatter(coarse_local, 'col', scatter_dimension=0, tiled=True)]
    scatter-add x1 -> x0, other arithmetic: 31.5 us -> none  [per_device(): jax.ops.segment_sum(contribution.reshape(slot_total, coarse_size, coarse_...]
    gather x4 -> x0, local copies, waits for them, and re-layouts: 29.6 us -> none  [the longest x1 11.1 us: per_device(): prolong_table[tile_index]]
    dot_general x2 -> x0, matrix products: 21.2 us -> none  [the longest x1 11.1 us: per_device(): jnp.einsum('rad,rkae->rkde', prolong, applied, preferred_element_type=jnp...]
    all_to_all x1 -> x0, blocking collectives: 19.3 us -> none  [per_device(): lax.all_to_all(requests, 'space', split_axis=0, concat_axis=0, tiled=True)]
  transfers between devices with their start and end apart: 4 -> 0, of which waited for: 4 -> 0; matrix products, arithmetic and copies ran while one was open for 0% -> 0% of each run, Pallas kernels for 0% -> 0%
where the time goes in v1:
time: 229 us; the launch traced here: 228 us
  Pallas kernels  220 us (96%)
  local copies, waits for them, and re-layouts  5.43 us (2%)
  other arithmetic  3.14 us (1%)
    pallas_call x1, Pallas kernels, per_device(): pl.pallas_call(functools.partial(kernel, (rows, slots, n_local)), out_sha...  220 us

profile of v1, /device:TPU:6, one launch (start us, length us, event | category | flops | bytes accessed | tf_op | source)
XLA Modules:
  0.0 228.4 jit_solution(10788544423398503491)
XLA Ops:
  0.0 0.7 broadcast_multiply_fusion
  0.7 0.7 broadcast_add_fusion
  1.3 0.7 broadcast_compare_fusion
  2.1 0.2 lt.80
  2.2 0.1 copy.14
  2.3 0.2 lt.88
  2.5 0.8 copy.12
  3.3 0.2 reshape.318
  3.5 0.2 fusion.2
  3.7 0.3 convert_reduce_fusion
  4.0 0.1 convert_reduce_fusion.2
  4.1 0.1 fusion.9
  4.3 0.8 copy.13
  5.0 0.2 reshape.319
  5.2 0.1 select_reduce_fusion.1
  5.3 0.1 select_reduce_fusion
  5.5 0.7 concatenate.3.tab
  6.1 0.1 and.221
  6.3 0.7 broadcast_in_dim.74.req
  6.9 219.8 %galerkin_step.1 = f32[5,128,128]{2,1,0:T(8,128)} custom-call(s32[896]{0:T(1024)} %concatenate.3.tab, s32[32,8,128]{2,1,0:T(8,128)} %broadcast_in_dim.74.req, f32[80,1,128]{2,1,0:T(1,128)} %bitcast.5, bf16[240,128,128]{2,1,0:T(8,128)(2,1)} %bitcast.4, bf16[80,128,128]{2,1,0:T(8,128)(2,1)} %basis_hbm.1), custom_call_target="tpu_custom_call" | custom-call | tf_op jit(solution)/shard_map/galerkin_step/pallas_call | solution.py:498
  226.7 1.7 copy.16
  (7 shorter events, 0.1 us)

commit v2 on v1

v2 whole, which is shorter than its diff:
```python
import functools

import jax
import jax.numpy as jnp
from jax import lax
from jax.experimental import pallas as pl
from jax.experimental.pallas import tpu as pltpu
from jax.sharding import PartitionSpec as P

KC = 4
CAP = 3
NCD = 10
NX, NZ, NY = 4, 8, 4
MESH = pl.DeviceIdType.MESH
F32 = jnp.float32
BF16 = jnp.bfloat16
HALF = 64
S_WIRE = BF16
C_WIRE = BF16


def dot_nt(a, b):
    return lax.dot_general(a, b, (((1,), (1,)), ((), ())), preferred_element_type=F32)


def step_offset(o):
    zi, xi = o // NX, o % NX
    hz, hx = (zi + 1) // 2, (xi + 1) // 2
    dz = ((zi % 2) * hz + (1 - zi % 2) * (NZ - hz)) % NZ
    dx = ((xi % 2) * hx + (1 - xi % 2) * (NX - hx)) % NX
    return dx, dz


def kernel(
    sizes,
    fields,
    weights,
    blocks_hbm,
    basis_hbm,
    out,
    blocks,
    basis,
    table,
    ptab,
    req,
    tab_v,
    tab,
    asked_v,
    asked,
    stage,
    recv1,
    recv2,
    big,
    total,
    coarse_t,
    xs,
    xr,
    s1,
    r1,
    s2,
    r2,
    xs_f,
    xr_f,
    s1_f,
    r1_f,
    s2_f,
    r2_f,
    load_sem,
    req_send,
    req_recv,
    a_send,
    a_recv,
    b_send,
    b_recv,
    rs_send,
    rs_recv,
    rf_send,
    rf_recv,
    ag_send,
    ag_recv,
):
    rows, slots, n_local = sizes
    space_count = NX * NZ
    peers = space_count - 1
    own_rows = rows // (2 * NY)
    n_remote = slots - n_local
    r_base = rows
    c_base = n_local
    g_base = n_local + space_count * CAP

    me = lax.axis_index("space")
    col = lax.axis_index("col")
    mx, mz = me // NZ, me % NZ
    my, core = col // 2, col % 2
    ya = my + 1 - 2 * (my % 2)
    yb = NY - 1 - my
    yo = (my + 2) % NY
    dev_x = (me, my * 2 + 1 - core)
    dev_a = (me, ya * 2 + core)
    dev_b = (me, yb * 2 + core)

    def target(o):
        dx, dz = step_offset(o)
        return (((mx + dx) % NX) * NZ + (mz + dz) % NZ, col)

    def origin(o):
        dx, dz = step_offset(o)
        return (((mx + NX - dx) % NX) * NZ + (mz + NZ - dz) % NZ, col)

    load_a = pltpu.make_async_copy(blocks_hbm, blocks, load_sem.at[0])
    load_b = pltpu.make_async_copy(basis_hbm, basis, load_sem.at[1])
    load_b.start()
    load_a.start()

    barrier = pltpu.get_barrier_semaphore()

    def greet(o, carry):
        pl.semaphore_signal(barrier, 1, device_id=target(o), device_id_type=MESH)
        return carry

    lax.fori_loop(1, space_count, greet, 0)
    for peer in (dev_x, dev_a, dev_b):
        pl.semaphore_signal(barrier, 1, device_id=peer, device_id_type=MESH)
    zero_b = jnp.zeros((2, HALF, 128), BF16)
    zero_f = jnp.zeros((2, HALF, 128), F32)
    table[rows] = zero_b
    ptab[0, rows] = zero_b[0]
    ptab[1, rows] = zero_b[0]
    big[r_base] = zero_f
    big[c_base] = zero_f

    cols = fields[...]
    lines = cols.T

    def col_of(m, k):
        return m[:, k : k + 1]

    def line_of(m, k):
        return m[k : k + 1, :]

    def fold(m):
        return jnp.sum(m.astype(jnp.int32), axis=0, keepdims=True)

    sub = lax.broadcasted_iota(jnp.int32, (128, 128), 0)
    lane = lax.broadcasted_iota(jnp.int32, (128, 128), 1)
    lane_row = lax.broadcasted_iota(jnp.int32, (1, 128), 1)
    sub_col = lax.broadcasted_iota(jnp.int32, (128, 1), 0)
    prior = sub < lane
    blank = jnp.zeros((1, 128), jnp.int32)

    def ahead(same, less, k, k2):
        if k2 < k:
            return same | less
        if k2 > k:
            return less
        return (same & prior) | less

    none = jnp.zeros((128, 128), jnp.bool_)
    bucket_line = []
    for k in range(3):
        step = line_of(lines, k)
        position = blank
        for k2 in range(3):
            same = col_of(cols, k2) == step
            position = position + fold(ahead(same, none, k, k2))
        bucket_line.append(jnp.where(step > 0, step * CAP + position, 0))

    def upright(rows_):
        return jnp.concatenate(
            rows_ + [jnp.zeros((128 - len(rows_), 128), jnp.int32)], axis=0
        ).T

    bucket = upright(bucket_line)
    packed = blank
    for k in range(3):
        match = (col_of(bucket, k) == lane) & (col_of(cols, k) > 0)
        packed = packed + fold(
            jnp.where(match, col_of(cols, 3 + k) + 128 * (3 * sub_col + k), 0)
        )
    req[0] = packed & 127
    pl.semaphore_wait(barrier, peers + 3)

    def remote(src, dst, send, recv, dev):
        return pltpu.make_async_remote_copy(
            src, dst, send, recv, device_id=dev, device_id_type=MESH
        )

    def ask(o):
        return remote(req, asked_v.at[o], req_send.at[o], req_recv.at[o], origin(o))

    def ask_start(o, carry):
        ask(o).start()
        return carry

    lax.fori_loop(1, space_count, ask_start, 0)
    live = [line_of(lines, 9 + k) for k in range(3)]
    for k in range(3):
        local_tile = jnp.where(
            (line_of(lines, k) == 0) & (live[k] > 0), line_of(lines, 3 + k), rows
        )
        tab_v[k : k + 1, :] = local_tile
        tab_v[3 + k : 4 + k, :] = jnp.where(live[k] > 0, bucket_line[k], 0)
    tab_v[6:7, :] = packed >> 7
    code_line, place_line = [], []
    for k in range(3):
        step = line_of(lines, k)
        goal = line_of(lines, 6 + k)
        rank, again = blank, blank
        for k2 in range(3):
            kind = (
                ((col_of(cols, k2) > 0) & (step > 0)) | ((col_of(cols, k2) == 0) & (step == 0))
            )
            same = (col_of(cols, 6 + k2) == goal) & kind
            less = (col_of(cols, 6 + k2) < goal) & kind
            rank = rank + fold(ahead(same, less, k, k2))
            again = again + fold(ahead(same, none, k, k2))
        keep_bit = jnp.where(again > 0, 1 << 15, 0)
        code_line.append(
            keep_bit
            + jnp.where(
                step > 0,
                tab_v[3 + k : 4 + k, :],
                jnp.minimum(3 * lane_row + k, slots - 1) + 256 * tab_v[k : k + 1, :],
            )
        )
        place_line.append(
            jnp.where(step > 0, 256 + rank, jnp.where(step == 0, rank, 1024))
        )
    sorted_cols = upright(code_line + place_line)
    for part in range(3):
        listed = blank
        for k in range(3):
            listed = listed + fold(
                jnp.where(
                    col_of(sorted_cols, 3 + k) == lane + 128 * part, col_of(sorted_cols, k), 0
                )
            )
        tab_v[7 + part : 8 + part, :] = listed
    for kind_at, first, size in ((10, 0, n_local), (11, g_base, n_remote)):
        count, some = blank, blank
        for k in range(3):
            mine = (col_of(cols, k) > 0) if first else (col_of(cols, k) == 0)
            goal = col_of(cols, 6 + k)
            count = count + fold((goal <= lane) & mine)
            some = some + fold((goal == lane) & mine)
        tab_v[kind_at : kind_at + 1, :] = jnp.where(
            some > 0, first + jnp.minimum(count, size) - 1, c_base
        )
    tab_copy = pltpu.make_async_copy(tab_v, tab, load_sem.at[3])
    tab_copy.start()
    load_b.wait()

    def flip(i, carry):
        table[i] = basis[i].T.reshape(2, HALF, 128)
        return carry

    lax.fori_loop(0, rows, flip, 0, unroll=2)

    def ask_wait(o, carry):
        ask(o).wait()
        return carry

    lax.fori_loop(1, space_count, ask_wait, 0)
    to_scalar = pltpu.make_async_copy(
        asked_v.at[pl.ds(1, peers)], asked.at[pl.ds(1, peers)], load_sem.at[2]
    )
    to_scalar.start()
    to_scalar.wait()
    tab_copy.wait()

    def held(value, last):
        return jnp.minimum(jnp.maximum(value, 0), last)

    def halo(recv, send_sem, recv_sem, h, o):
        return remote(
            stage.at[h, o],
            recv.at[h, o],
            send_sem.at[h * space_count + o],
            recv_sem.at[h * space_count + o],
            target(o),
        )

    halo1 = functools.partial(halo, recv1, a_send, a_recv)
    halo2 = functools.partial(halo, recv2, b_send, b_recv)

    def each_peer(body):
        def step(o, carry):
            body(o)
            return carry

        lax.fori_loop(1, space_count, step, 0)

    def send1(h):
        def one(o):
            for j in range(CAP):
                stage[h, o, j] = table[held(asked[o, 0, 0, o * CAP + j], rows), h]
            halo1(h, o).start()

        each_peer(one)

    send1(0)
    load_a.wait()

    def local_smooth(i, carry):
        lhs = jnp.concatenate(
            [table[held(tab[k, i], rows)].reshape(128, 128) for k in range(3)], axis=1
        )
        rhs = jnp.concatenate([blocks[3 * i + k] for k in range(3)], axis=1)
        big[i] = dot_nt(lhs, rhs).reshape(2, HALF, 128)
        return carry

    lax.fori_loop(0, rows, local_smooth, 0, unroll=2)
    send1(1)

    def remote_smooth(h):
        def one(o):
            halo1(h, o).wait_recv()
            for j in range(CAP):
                big[r_base + o * CAP + j, h] = dot_nt(
                    recv1[h, o, j], blocks[held(tab[6, o * CAP + j], slots - 1)]
                )

        each_peer(one)

    def reduce_scatter(n, part, xs, xr, s1, r1, s2, r2, send, recv, base):
        groups = (ya, yb, yo, my)
        h1 = (n + 1) // 2
        h2 = n - h1
        kind = xs.dtype

        def swap(i):
            return remote(
                xs.at[pl.ds(i * n, n)],
                xr.at[pl.ds(i * n, n)],
                send.at[base + i],
                recv.at[base + i],
                dev_x,
            )

        for i in range(4):

            def fill(t, carry):
                xs[i * n + t] = part((groups[i] * 2 + 1 - core) * n + t).astype(kind)
                return carry

            lax.fori_loop(0, n, fill, 0, unroll=n)
            swap(i).start()
        for i in range(4):

            def keep(t, carry):
                total[i * n + t] = part((groups[i] * 2 + core) * n + t)
                return carry

            lax.fori_loop(0, n, keep, 0, unroll=n)

        def hop(src, dst, at, size, sem, dev):
            return remote(
                src.at[pl.ds(at, size)],
                dst.at[pl.ds(at, size)],
                send.at[base + sem],
                recv.at[base + sem],
                dev,
            )

        m0 = hop(s1, r1, 0, h1, 4, dev_a)
        m1 = hop(s1, r1, h1, h1, 5, dev_a)
        m2 = hop(s1, r1, 2 * h1, h2, 6, dev_b)
        m3 = hop(s1, r1, 2 * h1 + h2, h2, 7, dev_b)
        m4 = hop(s2, r2, 0, h1, 8, dev_b)
        m5 = hop(s2, r2, h1, h2, 9, dev_a)

        def add_swapped(i):
            swap(i).wait_recv()
            for t in range(n):
                total[i * n + t] += xr[i * n + t].astype(F32)

        def put(dst, at, first, size):
            for t in range(size):
                dst[at + t] = total[first + t].astype(kind)

        def take(src, at, first, size):
            for t in range(size):
                total[first + t] += src[at + t].astype(F32)

        add_swapped(0)
        put(s1, 0, 0, h1)
        m0.start()
        add_swapped(1)
        put(s1, 2 * h1, n + h1, h2)
        m2.start()
        add_swapped(2)
        put(s1, h1, 2 * n, h1)
        m1.start()
        put(s1, 2 * h1 + h2, 2 * n + h1, h2)
        m3.start()
        add_swapped(3)
        m1.wait_recv()
        take(r1, h1, n, h1)
        put(s2, 0, n, h1)
        m4.start()
        m3.wait_recv()
        take(r1, 2 * h1 + h2, h1, h2)
        put(s2, h1, h1, h2)
        m5.start()
        m0.wait_recv()
        take(r1, 0, 3 * n, h1)
        m2.wait_recv()
        take(r1, 2 * h1, 3 * n + h1, h2)
        m4.wait_recv()
        take(r2, 0, 3 * n, h1)
        m5.wait_recv()
        take(r2, h1, 3 * n + h1, h2)

        def drain():
            for i in range(4):
                swap(i).wait_send()
            for m in (m0, m1, m2, m3, m4, m5):
                m.wait_send()

        return drain

    n = own_rows
    n1 = (n + 1) // 2
    n2 = n - n1
    other = 1 - core

    def make_prolong(h):
        def smooth_part(row):
            acc = big[row, h]
            for k in range(3):
                acc = acc + big[r_base + held(tab[3 + k, row], space_count * CAP - 1), h]
            return acc

        reduce_scatter(
            n, smooth_part, xs, xr, s1, r1, s2, r2, rs_send, rs_recv, 10 * h
        )()
        for t in range(n):
            row = col * n + t
            ptab[h, row] = (table[row, h].astype(F32) - weights[row] * total[3 * n + t]).astype(
                BF16
            )

        def spread(y, at, size, sem, dev):
            region = ptab.at[h, pl.ds((y * 2 + core) * n + at, size)]
            return remote(region, region, ag_send.at[9 * h + sem], ag_recv.at[9 * h + sem], dev)

        def arrive(y, c, at, size, sem):
            region = ptab.at[h, pl.ds((y * 2 + c) * n + at, size)]
            remote(
                region, region, ag_send.at[9 * h + sem], ag_recv.at[9 * h + sem], dev_x
            ).wait_recv()

        sent = []

        def go(*args):
            copy = spread(*args)
            copy.start()
            sent.append(copy)

        go(my, 0, n, 0, dev_a)
        go(my, 0, n, 1, dev_b)
        go(my, 0, n, 2, dev_x)
        arrive(ya, core, 0, n, 0)
        go(ya, 0, n1, 3, dev_b)
        go(ya, 0, n, 5, dev_x)
        arrive(yb, core, 0, n, 1)
        go(yb, n1, n2, 4, dev_a)
        go(yb, 0, n, 6, dev_x)
        arrive(yo, core, 0, n1, 3)
        go(yo, 0, n1, 7, dev_x)
        arrive(yo, core, n1, n2, 4)
        go(yo, n1, n2, 8, dev_x)
        arrive(my, other, 0, n, 2)
        arrive(ya, other, 0, n, 5)
        arrive(yb, other, 0, n, 6)
        arrive(yo, other, 0, n1, 7)
        arrive(yo, other, n1, n2, 8)
        return sent

    def send2(h):
        def one(o):
            halo1(h, o).wait_send()
            for j in range(CAP):
                stage[h, o, j] = ptab[h, held(asked[o, 0, 0, o * CAP + j], rows)]
            halo2(h, o).start()

        each_peer(one)

    for h in range(2):
        remote_smooth(h)
        sent = make_prolong(h)
        send2(h)
        for copy in sent:
            copy.wait_send()

    def whole(row):
        return jnp.concatenate([ptab[0, row], ptab[1, row]], axis=0)

    def galerkin(slot, tile):
        applied = dot_nt(tile, blocks[slot]).astype(BF16)
        return dot_nt(applied, whole(lax.div(slot, 3)))

    group = 4

    def local_galerkin(b, acc):
        parts = []
        for u in range(group):
            q = b * group + u
            code = tab[7 + q // 128, q % 128]
            parts.append((code >> 15, galerkin(held(code & 255, slots - 1), whole(held((code >> 8) & 127, rows)))))
        for u, (keep, c) in enumerate(parts):
            acc = jnp.where(keep > 0, acc, 0.0) + c
            big[b * group + u] = acc.reshape(2, HALF, 128)
        return acc

    lax.fori_loop(0, n_local // group, local_galerkin, jnp.zeros((128, 128), F32))

    n_out = NCD * KC // (2 * NY)

    def finish(h):
        def one(o):
            halo2(h, o).wait_recv()
            for j in range(CAP):
                big[c_base + o * CAP + j, h] = galerkin(
                    held(tab[6, o * CAP + j], slots - 1), recv2[h, o, j]
                )

        each_peer(one)

        def remote_sum(q, acc):
            code = tab[9, q]
            acc = jnp.where((code >> 15) > 0, acc, 0.0) + big[c_base + held(code & 127, space_count * CAP - 1), h]
            big[g_base + q, h] = acc
            return acc

        lax.fori_loop(0, n_remote, remote_sum, jnp.zeros((HALF, 128), F32), unroll=4)

        def coarse_part(t):
            end = big.shape[0] - 1
            return big[held(tab[10, t], end), h] + big[held(tab[11, t], end), h]

        bufs = [b.at[h] for b in (xs_f, xr_f, s1_f, r1_f, s2_f, r2_f)]
        drain = reduce_scatter(n_out, coarse_part, *bufs, rf_send, rf_recv, 10 * h)
        for t in range(n_out):
            coarse_t[t, h] = total[3 * n_out + t]
        return drain

    drains = [finish(h) for h in range(2)]
    for t in range(n_out):
        out[t] = coarse_t[t].reshape(128, 128).T
    for h in range(2):
        each_peer(lambda o: halo2(h, o).wait_send())
        drains[h]()


def ring_rank(delta, size):
    return jnp.where(delta == 0, 0, jnp.where(2 * delta <= size, 2 * delta - 1, 2 * (size - delta)))


def per_device(
    blocks, basis_tiles, weights, neighbour_device, neighbour_row, counts, aggregate, pair_slot
):
    own = lax.axis_index("space")
    col = lax.axis_index("col")
    space_count = lax.axis_size("space")
    rows, slot_count = neighbour_device.shape
    slots = rows * slot_count
    n_remote = 60
    n_local = slots - n_remote
    live = (
        col * slot_count + jnp.arange(slot_count, dtype=jnp.int32)[None, :] < counts[:, None]
    )
    target = aggregate[:, None] * KC + pair_slot
    step = ring_rank((own % NZ - neighbour_device % NZ) % NZ, NZ) * NX + ring_rank(
        (own // NZ - neighbour_device // NZ) % NX, NX
    )
    fields = jnp.concatenate(
        [step, neighbour_row, target, live.astype(jnp.int32)], axis=1
    )
    fields = jnp.pad(
        fields, ((0, 128 - rows), (0, 128 - 4 * slot_count)), constant_values=-1
    )
    own_rows = rows // (2 * NY)
    n_out = NCD * KC // (2 * NY)
    tile = (128, 128)
    half = (HALF, 128)

    def rs_buffers(lead, n, kind):
        return [pltpu.VMEM(lead + (m * n,) + half, kind) for m in (4, 4, 2, 2, 1, 1)]

    dma = pltpu.SemaphoreType.DMA
    return pl.pallas_call(
        functools.partial(kernel, (rows, slots, n_local)),
        out_shape=jax.ShapeDtypeStruct((n_out,) + tile, F32),
        in_specs=[
            pl.BlockSpec(memory_space=pltpu.VMEM),
            pl.BlockSpec(memory_space=pltpu.VMEM),
            pl.BlockSpec(memory_space=pl.ANY),
            pl.BlockSpec(memory_space=pl.ANY),
        ],
        out_specs=pl.BlockSpec(memory_space=pltpu.VMEM),
        scratch_shapes=[
            pltpu.VMEM((slots,) + tile, BF16),
            pltpu.VMEM((rows,) + tile, BF16),
            pltpu.VMEM((rows + 1, 2) + half, BF16),
            pltpu.VMEM((2, rows + 1) + half, BF16),
            pltpu.VMEM((1, 1, 128), jnp.int32),
            pltpu.VMEM((16, 128), jnp.int32),
            pltpu.SMEM((16, 128), jnp.int32),
            pltpu.VMEM((space_count, 1, 1, 128), jnp.int32),
            pltpu.SMEM((space_count, 1, 1, 128), jnp.int32),
            pltpu.VMEM((2, space_count, CAP) + half, BF16),
            pltpu.VMEM((2, space_count, CAP) + half, BF16),
            pltpu.VMEM((2, space_count, CAP) + half, BF16),
            pltpu.VMEM((n_local + space_count * CAP + n_remote, 2) + half, F32),
            pltpu.VMEM((4 * own_rows,) + half, F32),
            pltpu.VMEM((n_out, 2) + half, F32),
            *rs_buffers((), own_rows, S_WIRE),
            *rs_buffers((2,), n_out, C_WIRE),
            dma((4,)),
            *([dma((space_count,))] * 2),
            *([dma((2 * space_count,))] * 4),
            *([dma((20,))] * 4),
            *([dma((18,))] * 2),
        ],
        compiler_params=pltpu.CompilerParams(
            collective_id=0, has_side_effects=True, vmem_limit_bytes=62 << 20
        ),
        name="galerkin_step",
    )(
        fields,
        weights.reshape(rows, 1, 128),
        blocks.reshape((slots,) + tile),
        basis_tiles,
    )


def solution(mesh):
    return jax.shard_map(
        per_device,
        mesh=mesh,
        in_specs=(
            P("space", "col", None, None),
            P("space", None, None),
            P("space", None),
            P("space", "col"),
            P("space", "col"),
            P("space"),
            P("space"),
            P("space", "col"),
        ),
        out_specs=P(("space", "col"), None, None),
        check_vma=False,
    )
```

time: 229 us -> 184 us (0.80)
  Pallas kernels: 220 us -> 177 us
  local copies, waits for them, and re-layouts: 5.43 us -> 2.46 us
    pallas_call x1, Pallas kernels: 220 us -> 177 us  [per_device(): pl.pallas_call(functools.partial(kernel, (rows, slots, n_local)), out_sha...]
where the time goes in v2:
time: 184 us; the launch traced here: 182 us
  Pallas kernels  177 us (96%)
  other arithmetic  2.8 us (2%)
  local copies, waits for them, and re-layouts  2.46 us (1%)
    pallas_call x1, Pallas kernels, per_device(): pl.pallas_call(functools.partial(kernel, (rows, slots, n_local)), out_sha...  177 us

profile of v2, /device:TPU:6, one launch (start us, length us, event | category | flops | bytes accessed | tf_op | source)
XLA Modules:
  0.0 181.8 jit_solution(14234074886295965879)
XLA Ops:
  0.0 0.7 broadcast_multiply_fusion
  0.7 0.7 compare_convert_fusion
  1.4 0.7 select_add_fusion
  2.1 0.7 pad_add_fusion
  2.8 0.1 copy.19
  2.9 0.6 pad.4.fields
  3.5 176.5 %galerkin_step.1 = f32[5,128,128]{2,1,0:T(8,128)} custom-call(s32[128,128]{1,0:T(8,128)} %pad.4.fields, f32[80,1,128]{2,1,0:T(1,128)} %bitcast.3, bf16[240,128,128]{2,1,0:T(8,128)(2,1)} %bitcast.2, bf16[80,128,128]{2,1,0:T(8,128)(2,1)} %basis_hbm.1), custom_call_target="tpu_custom_call" | custom-call | tf_op jit(solution)/shard_map/galerkin_step/pallas_call | solution.py:592
  180.1 1.7 copy.21
  (1 shorter events, 0.0 us)

commit v3 on v2

--- a/solution.py
+++ b/solution.py
@@ -52,7 +52,6 @@
     recv2,
     big,
     total,
-    coarse_t,
     xs,
     xr,
     s1,
@@ -535,22 +534,23 @@
 
         lax.fori_loop(0, n_remote, remote_sum, jnp.zeros((HALF, 128), F32), unroll=4)
 
-        def coarse_part(t):
-            end = big.shape[0] - 1
-            return big[held(tab[10, t], end), h] + big[held(tab[11, t], end), h]
-
-        bufs = [b.at[h] for b in (xs_f, xr_f, s1_f, r1_f, s2_f, r2_f)]
-        drain = reduce_scatter(n_out, coarse_part, *bufs, rf_send, rf_recv, 10 * h)
-        for t in range(n_out):
-            coarse_t[t, h] = total[3 * n_out + t]
-        return drain
-
-    drains = [finish(h) for h in range(2)]
+    for h in range(2):
+        finish(h)
+
+    def coarse_part(r):
+        t, h = r // 2, r % 2
+        end = big.shape[0] - 1
+        return big[held(tab[10, t], end), h] + big[held(tab[11, t], end), h]
+
+    drain = reduce_scatter(
+        2 * n_out, coarse_part, xs_f, xr_f, s1_f, r1_f, s2_f, r2_f, rf_send, rf_recv, 0
+    )
     for t in range(n_out):
-        out[t] = coarse_t[t].reshape(128, 128).T
+        at = 6 * n_out + 2 * t
+        out[t] = jnp.concatenate([total[at], total[at + 1]], axis=0).T
     for h in range(2):
         each_peer(lambda o: halo2(h, o).wait_send())
-        drains[h]()
+    drain()
 
 
 def ring_rank(delta, size):
@@ -614,9 +614,8 @@
             pltpu.VMEM((2, space_count, CAP) + half, BF16),
             pltpu.VMEM((n_local + space_count * CAP + n_remote, 2) + half, F32),
             pltpu.VMEM((4 * own_rows,) + half, F32),
-            pltpu.VMEM((n_out, 2) + half, F32),
             *rs_buffers((), own_rows, S_WIRE),
-            *rs_buffers((2,), n_out, C_WIRE),
+            *rs_buffers((), 2 * n_out, C_WIRE),
             dma((4,)),
             *([dma((space_count,))] * 2),
             *([dma((2 * space_count,))] * 4),

time: 184 us -> 182 us (0.989); the launches traced: 182 us -> 182 us
  no operation moved by 1% of the time
where the time goes in v3:
time: 182 us
  Pallas kernels  177 us (97%)
  other arithmetic  2.8 us (2%)
  local copies, waits for them, and re-layouts  2.46 us (1%)
    pallas_call x1, Pallas kernels, per_device(): pl.pallas_call(functools.partial(kernel, (rows, slots, n_local)), out_sha...  177 us

profile of v3, /device:TPU:6, one launch (start us, length us, event | category | flops | bytes accessed | tf_op | source)
XLA Modules:
  0.0 181.8 jit_solution(2669399057326633829)
XLA Ops:
  0.0 0.7 broadcast_multiply_fusion
  0.7 0.7 compare_convert_fusion
  1.4 0.7 select_add_fusion
  2.1 0.7 pad_add_fusion
  2.8 0.1 copy.19
  2.9 0.6 pad.4.fields
  3.5 176.6 %galerkin_step.1 = f32[5,128,128]{2,1,0:T(8,128)} custom-call(s32[128,128]{1,0:T(8,128)} %pad.4.fields, f32[80,1,128]{2,1,0:T(1,128)} %bitcast.3, bf16[240,128,128]{2,1,0:T(8,128)(2,1)} %bitcast.2, bf16[80,128,128]{2,1,0:T(8,128)(2,1)} %basis_hbm.1), custom_call_target="tpu_custom_call" | custom-call | tf_op jit(solution)/shard_map/galerkin_step/pallas_call | solution.py:592
  180.1 1.7 copy.21
  (1 shorter events, 0.0 us)
